TPU v7x, 32 devices: a whole 2x2x4 slice. The times are simulated.
32 devices in a mesh: tile: 32 (over z, y, x, core), lev: 1.
Axes of the slice: x: 2, y: 2, z: 4, core: 2. Of those that a mesh axis runs over, the one named last changes fastest.
Arguments:
- cotangent: float32 [24, 4, 64, 900], P('lev', None, 'tile'), may hold values from -6 to 6
- courant_x: float32 [24, 64, 900], P('lev', 'tile'), may hold values from -0.6 to 0.6
- courant_y: float32 [24, 64, 900], P('lev', 'tile'), may hold values from -0.6 to 0.6
- diffusivity: float32 [64, 900], P('tile'), may hold values from 0.04 to 0.16
- vert_diff: float32 [24, 64, 900], P('lev', 'tile'), may hold values from 0.5 to 2000
- level_count: int32 [64, 900], P('tile'), may hold values from 0 to 24
- edge_tile: int32 [64, 4], P('tile'), may hold values from -1 to 63, as said below
- edge_code: int32 [64, 4], P('tile'), may hold values from 0 to 7
- corner_tile: int32 [64, 4], P('tile'), may hold values from -1 to 63, as said below
- corner_code: int32 [64, 4], P('tile'), may hold values from 0 to 3
Outputs:
- tracer_adjoint: float32 [24, 4, 64, 900], P('lev', None, 'tile')
Inputs may be any that keep to these rules, and one draw needn't show every extreme that they name: Side lists are symmetric: if edge_tile[t, s] = q and edge_code[t, s] = e + 4 r, then edge_tile[q, e] = t and edge_code[q, e] = s + 4 r. Every partner q satisfies min(|q - t|, 64 - |q - t|) <= 16. Sides at the band's rim and sides towards land are -1. Corner lists are symmetric: if corner_tile[t, c] = q and corner_code[t, c] = k, then corner_tile[q, k] = t and corner_code[q, k] = c. Every partner q satisfies min(|q - t|, 64 - |q - t|) <= 16.
All inputs are finite; a program needn't handle non-finite values.
Results may differ from a plain program's by a relative error of at most 0.0003.
Values sent between devices are 32-bit elements; how exact they have to be, the bound alone decides.
A program may use at most 128 MiB of HBM per device.

v0:
```python
import functools

import jax
import jax.numpy as jnp
import numpy as np
from jax import lax
from jax.experimental import pallas as pl
from jax.experimental.pallas import tpu as pltpu
from jax.sharding import PartitionSpec as P

EDGE = 30
BAND = 8


stencil_offsets = [(0, -1), (0, 1), (-1, 0), (1, 0), (-1, -1), (-1, 1), (1, -1), (1, 1)]


def from_behind(value, axis, steps):
    count = lax.axis_size(axis)
    initial, last = (max(0, -steps), min(count, count - steps))
    return lax.ppermute(value, axis, [(source, source + steps) for source in range(initial, last)])


def shifted_2(value, axis, by):
    devices = lax.axis_size(axis)
    return lax.ppermute(value, axis, [(i, (i + by) % devices) for i in range(devices)])


def stencil_weights(diffuse, flow_x, flow_y):
    return [
        diffuse + 0.5 * flow_x,
        diffuse - 0.5 * flow_x,
        diffuse + 0.5 * flow_y,
        diffuse - 0.5 * flow_y,
        0.25 * diffuse,
        0.25 * diffuse,
        0.25 * diffuse,
        0.25 * diffuse,
    ]


def eliminate(right_side, coupling_up, coupling_down, initial):

    def advance(state, inputs):
        factor, partial_value = state
        source, upper_term, lower_term = inputs
        divisor = 1.0 + upper_term + lower_term + upper_term * factor
        factor_new = -lower_term / divisor
        partial_new = (source + upper_term * partial_value) / divisor
        return ((factor_new, partial_new), (factor_new, partial_new))

    final_state, outputs = lax.scan(advance, initial, (right_side, coupling_up, coupling_down))
    return outputs


def substitute(factors, partials, below_field):

    def backward(state, inputs):
        factor, partial_value = inputs
        column_value = partial_value - factor * state
        return (column_value, column_value)

    final_state, fields = lax.scan(backward, below_field, (factors, partials), reverse=True)
    return fields


def cycle_tables():
    padded_edge = EDGE + 2
    cycle_spots = []
    cell_spots = []
    for border in range(4):
        for position in range(EDGE):
            if border == 0:
                cycle_spots.append(position + 1)
                cell_spots.append(position)
            elif border == 1:
                cycle_spots.append((padded_edge - 1) * padded_edge + position + 1)
                cell_spots.append((EDGE - 1) * EDGE + position)
            elif border == 2:
                cycle_spots.append((position + 1) * padded_edge)
                cell_spots.append(position * EDGE)
            else:
                cycle_spots.append((position + 1) * padded_edge + padded_edge - 1)
                cell_spots.append(position * EDGE + EDGE - 1)
    cycle_spots += [
        0,
        padded_edge - 1,
        (padded_edge - 1) * padded_edge,
        padded_edge * padded_edge - 1,
    ]
    cell_spots += [0, EDGE - 1, (EDGE - 1) * EDGE, EDGE * EDGE - 1]
    placing = np.zeros((len(cycle_spots), EDGE * EDGE), np.float32)
    placing[np.arange(len(cycle_spots)), np.array(cell_spots)] = 1.0
    return (np.array(cycle_spots, np.int32), placing)


def embed(field):
    leading = field.shape[:-1]
    square = field.reshape(leading + (EDGE, EDGE))
    padded = jnp.pad(square, [(0, 0)] * len(leading) + [(1, 1), (1, 1)])
    return padded.reshape(leading + ((EDGE + 2) * (EDGE + 2),))


def shards(
    cotangent,
    courant_x,
    courant_y,
    diffusivity,
    vert_diff,
    level_count,
    edge_tile,
    edge_code,
    corner_tile,
    corner_code,
):
    levels_here = cotangent.shape[0]
    tracers = cotangent.shape[1]
    tiles_here = cotangent.shape[2]
    cells = cotangent.shape[3]
    padded_edge = EDGE + 2
    cycle_size = 4 * EDGE + 4
    lev_count = lax.axis_size("lev")
    depth_index = (
        lax.axis_index("lev") * levels_here
        + jnp.arange(levels_here, dtype=jnp.int32)[:, None, None]
    )
    wet_mask = (depth_index < level_count[None]).astype(jnp.float32)
    coupling = jnp.where(depth_index == 0, jnp.float32(0.0), vert_diff * wet_mask)
    deeper = from_behind(coupling[0], "lev", -1)
    coupling_down = jnp.concatenate([coupling[1:], deeper[None]], axis=0)[:, None]
    coupling_up = coupling[:, None]
    initial = (
        jnp.zeros((1, tiles_here, cells), jnp.float32),
        jnp.zeros((tracers, tiles_here, cells), jnp.float32),
    )
    for sweep_index in range(lev_count - 1):
        factors, partials = eliminate(cotangent, coupling_up, coupling_down, initial)
        initial = from_behind((factors[-1], partials[-1]), "lev", 1)
    factors, partials = eliminate(cotangent, coupling_up, coupling_down, initial)
    below_field = jnp.zeros((tracers, tiles_here, cells), jnp.float32)
    for sweep_index in range(lev_count - 1):
        fields = substitute(factors, partials, below_field)
        below_field = from_behind(fields[0], "lev", -1)
    solved = substitute(factors, partials, below_field)
    weighted = solved * wet_mask[:, None]
    weighted_ext = embed(weighted)
    diffuse_ext = embed(diffusivity)[None, None]
    flow_x_ext = embed(courant_x)[:, None]
    flow_y_ext = embed(courant_y)[:, None]
    weights = stencil_weights(diffuse_ext, flow_x_ext, flow_y_ext)
    leading = weighted_ext.shape[:-1]
    spread = jnp.zeros_like(weighted_ext)
    for (shift_row, shift_col), weight in zip(stencil_offsets, weights):
        contribution = weight * weighted_ext
        offset = shift_row * padded_edge + shift_col
        if offset > 0:
            shifted = jnp.concatenate(
                [jnp.zeros(leading + (offset,), jnp.float32), contribution[..., :-offset]], axis=-1
            )
        else:
            shifted = jnp.concatenate(
                [contribution[..., -offset:], jnp.zeros(leading + (-offset,), jnp.float32)], axis=-1
            )
        spread = spread + shifted
    cycle_spots, placing = cycle_tables()
    outgoing = jnp.take(spread, jnp.asarray(cycle_spots), axis=3)
    interior = spread.reshape(leading + (padded_edge, padded_edge))[..., 1:-1, 1:-1].reshape(
        solved.shape
    )
    partners = jnp.concatenate([edge_tile, corner_tile], axis=1)

    def collect(gathered_sum, portion, first_tile):
        tile_span = portion.shape[2]
        onehot = (
            partners[:, :, None]
            == first_tile + jnp.arange(tile_span, dtype=jnp.int32)[None, None, :]
        ).astype(jnp.float32)
        return gathered_sum + jnp.einsum(
            "tkw,dnwr->dntkr", onehot, portion, precision=lax.Precision.HIGHEST
        )

    tile_count = lax.axis_size("tile")
    own_index = lax.axis_index("tile")
    reach = (2 * BAND + tiles_here - 1) // tiles_here
    fetched = collect(
        jnp.zeros((levels_here, tracers, tiles_here, 8, cycle_size), jnp.float32),
        outgoing,
        own_index * tiles_here,
    )
    for distance in range(-reach, reach + 1):
        if distance != 0:
            portion = shifted_2(outgoing, "tile", distance)
            source = (own_index - distance) % tile_count
            fetched = collect(fetched, portion, source * tiles_here)
    side_values = fetched[:, :, :, :4, : 4 * EDGE].reshape(
        levels_here, tracers, tiles_here, 4, 4, EDGE
    )
    side_choice = (
        (edge_code % 4)[:, :, None] == jnp.arange(4, dtype=jnp.int32)[None, None, :]
    ).astype(jnp.float32)
    strips = jnp.sum(side_values * side_choice[None, None, :, :, :, None], axis=4)
    strips = jnp.where((edge_code >= 4)[None, None, :, :, None], strips[..., ::-1], strips)
    corner_values = fetched[:, :, :, 4:, 4 * EDGE :]
    corner_choice = (
        corner_code[:, :, None] == jnp.arange(4, dtype=jnp.int32)[None, None, :]
    ).astype(jnp.float32)
    corner_picked = jnp.sum(corner_values * corner_choice[None, None], axis=4)
    arriving = jnp.concatenate(
        [strips.reshape(levels_here, tracers, tiles_here, 4 * EDGE), corner_picked], axis=3
    )
    returned = jnp.einsum(
        "dntr,rc->dntc", arriving, jnp.asarray(placing), precision=lax.Precision.HIGHEST
    )
    diffuse_here = diffusivity[None, None]
    return wet_mask[:, None] * ((1.0 - 5.0 * diffuse_here) * weighted + interior + returned)


PADDED = 1024
SIDE_LANES = 32
MESH = pl.DeviceIdType.MESH


def strip_selector():
    chosen = np.zeros((PADDED + 128, 256), np.float32)
    for j in range(EDGE):
        for side, lane in enumerate([PADDED - EDGE + j, EDGE * EDGE + j, EDGE * j, EDGE * j + EDGE - 1]):
            chosen[lane, SIDE_LANES * side + j] = 1.0
            chosen[lane, 128 + SIDE_LANES * side + EDGE - 1 - j] = 1.0
    for corner, cell in enumerate([0, EDGE - 1, (EDGE - 1) * EDGE, EDGE * EDGE - 1]):
        chosen[PADDED + cell % 128, SIDE_LANES * corner + EDGE] = 1.0
    return jnp.asarray(chosen, jnp.bfloat16)


def strip_placer():
    placing = np.zeros((128, PADDED), np.float32)
    for j in range(EDGE):
        for side, cell in enumerate([j, (EDGE - 1) * EDGE + j, EDGE * j, EDGE * j + EDGE - 1]):
            placing[SIDE_LANES * side + j, cell] = 1.0
    for corner, cell in enumerate([0, EDGE - 1, (EDGE - 1) * EDGE, EDGE * EDGE - 1]):
        placing[SIDE_LANES * corner + EDGE, cell] = 1.0
    return jnp.asarray(placing, jnp.bfloat16)


def split_dot(left, right):
    high = left.astype(jnp.bfloat16)
    low = (left - high.astype(jnp.float32)).astype(jnp.bfloat16)
    return jnp.dot(high, right, preferred_element_type=jnp.float32) + jnp.dot(
        low, right, preferred_element_type=jnp.float32
    )


def four_times(pair):
    return jnp.concatenate([pair, pair, pair, pair], axis=0)


def widen(rows):
    return jnp.concatenate(
        [rows, jnp.zeros((rows.shape[0], PADDED - rows.shape[1]), rows.dtype)], axis=1
    )


def solve_kernel(
    code_ref, cot_ref, cx_ref, cy_ref, dif_ref, vd_ref, lc_ref, sel_ref,
    base_ref, strips_ref, factor_ref, partial_ref, edge_ref,
):
    levels = cot_ref.shape[0]
    cells = cot_ref.shape[3]
    depth = four_times(lc_ref[...])

    def coupling(k):
        if k == 0 or k == levels:
            return jnp.zeros((8, cells), jnp.float32)
        return jnp.where(k < depth, four_times(vd_ref[k]), 0.0)

    factor = jnp.zeros((8, cells), jnp.float32)
    partial_value = jnp.zeros((8, cells), jnp.float32)
    upper = coupling(0)
    for k in range(levels):
        lower = coupling(k + 1)
        source = jnp.concatenate([cot_ref[k, n] for n in range(4)], axis=0)
        inverse = 1.0 / ((1.0 + upper + lower) + upper * factor)
        factor = -lower * inverse
        partial_value = (source + upper * partial_value) * inverse
        factor_ref[k] = factor
        partial_ref[k] = partial_value
        upper = lower

    lane = lax.broadcasted_iota(jnp.int32, (8, PADDED), 1)
    row_lane = jnp.where(lane >= PADDED - EDGE, lane - (PADDED - EDGE), lane)
    column = lax.rem(row_lane, EDGE)
    first = column == 0
    last = column == EDGE - 1
    inside = lane < cells
    short = lax.broadcasted_iota(jnp.int32, (8, 128), 1)
    corner_0 = (short == 0) | (short == EDGE - 1)
    corner_6 = short == ((EDGE - 1) * EDGE) % 128
    corner_7 = short == (EDGE * EDGE - 1) % 128
    diffuse = widen(four_times(dif_ref[...]))
    quarter = 0.25 * diffuse
    centre = 1.0 - 5.0 * diffuse
    wide_depth = widen(depth)
    solved = jnp.zeros((8, cells), jnp.float32)
    for k in reversed(range(levels)):
        solved = partial_ref[k] - factor_ref[k] * solved
        u = widen(jnp.where(k < depth, solved, 0.0))
        half_x = 0.5 * widen(four_times(cx_ref[k]))
        half_y = 0.5 * widen(four_times(cy_ref[k]))
        diagonal = quarter * u
        both = pltpu.roll(diagonal, EDGE, 1) + pltpu.roll(diagonal, PADDED - EDGE, 1)
        west = both + (diffuse + half_x) * u
        east = both + (diffuse - half_x) * u
        spread = pltpu.roll((diffuse + half_y) * u, PADDED - EDGE, 1)
        spread = spread + pltpu.roll((diffuse - half_y) * u, EDGE, 1)
        spread = spread + pltpu.roll(jnp.where(first, 0.0, west), PADDED - 1, 1)
        spread = spread + pltpu.roll(jnp.where(last, 0.0, east), 1, 1)
        base_ref[k] = jnp.where(k < wide_depth, centre * u + spread, 0.0)
        edge_ref[8 * k : 8 * k + 8, :PADDED] = jnp.where(
            inside, jnp.where(first, west, east), spread
        )
        edge_ref[8 * k : 8 * k + 8, PADDED:] = (
            jnp.where(corner_0, diagonal[:, 0:128], 0.0)
            + jnp.where(corner_6, diagonal[:, 768:896], 0.0)
            + jnp.where(corner_7, diagonal[:, 896:1024], 0.0)
        )
    both_ways = split_dot(edge_ref[...], sel_ref[...])
    parity = lax.rem(lax.broadcasted_iota(jnp.int32, (8, 128), 0), 2)
    code = jnp.zeros((8, 128), jnp.int32)
    for i in range(2):
        for side in range(4):
            code = jnp.where((parity == i) & (short // SIDE_LANES == side), code_ref[i, side], code)
    flipped = (code >= 4) & (lax.rem(short, SIDE_LANES) < EDGE)
    for k in range(levels):
        rows = both_ways[8 * k : 8 * k + 8]
        strips_ref[k] = jnp.where(flipped, rows[:, 128:], rows[:, :128])


def send_kernel(count, reach, strips_ref, near_ref, own_sem, send_sem, recv_sem):
    me = lax.axis_index("tile")
    barrier = pltpu.get_barrier_semaphore()
    offsets = [o for o in range(-reach, reach + 1) if o != 0]
    for o in offsets:
        pl.semaphore_signal(
            barrier, inc=1, device_id={"tile": lax.rem(me + o + count, count)}, device_id_type=MESH
        )
    own = pltpu.make_async_copy(strips_ref, near_ref.at[reach], own_sem)
    own.start()
    pl.semaphore_wait(barrier, len(offsets))
    copies = []
    for o in offsets:
        copy = pltpu.make_async_remote_copy(
            src_ref=strips_ref,
            dst_ref=near_ref.at[reach - o],
            send_sem=send_sem.at[reach + o],
            recv_sem=recv_sem.at[reach - o],
            device_id={"tile": lax.rem(me + o + count, count)},
            device_id_type=MESH,
        )
        copy.start()
        copies.append(copy)
    own.wait()
    for copy in copies:
        copy.wait()


def place_kernel(
    count, reach, et_ref, ec_ref, ct_ref, cc_ref, near_ref, base_ref, lc_ref, place_ref,
    out_ref, arriving_ref,
):
    levels = base_ref.shape[0]
    cells = out_ref.shape[3]
    me = lax.axis_index("tile")
    lane = lax.broadcasted_iota(jnp.int32, (8, 128), 1)
    parity = lax.rem(lax.broadcasted_iota(jnp.int32, (8, 128), 0), 2)
    group = lane // SIDE_LANES
    spot = lax.rem(lane, SIDE_LANES)
    total = jnp.zeros((levels, 8, 128), jnp.float32)
    for i in range(2):
        for tiles_ref, codes_ref, wanted in (
            (et_ref, ec_ref, spot < EDGE),
            (ct_ref, cc_ref, spot == EDGE),
        ):
            for side in range(4):
                tile = tiles_ref[i, side]
                there = jnp.maximum(tile, 0)
                slot = lax.rem(there // 2 - me + reach + count, count)
                slot = jnp.where(tile < 0, 0, slot)
                values = near_ref[slot]
                values = jnp.where(
                    lax.rem(there, 2) == i, values, pltpu.roll(values, 1 if i == 1 else 7, 1)
                )
                shift = lax.rem(SIDE_LANES * (side - lax.rem(codes_ref[i, side], 4)) + 128, 128)
                values = pltpu.roll(values, shift, 2)
                chosen = wanted & (group == side) & (parity == i) & (tile >= 0)
                total = jnp.where(chosen[None], values, total)
    for k in range(levels):
        arriving_ref[8 * k : 8 * k + 8] = total[k]
    returned = split_dot(arriving_ref[...], place_ref[...])
    depth = four_times(lc_ref[...])
    for k in range(levels):
        result = base_ref[k][:, :cells] + jnp.where(
            k < depth, returned[8 * k : 8 * k + 8, :cells], 0.0
        )
        for n in range(4):
            out_ref[k, n] = result[2 * n : 2 * n + 2]


def shards_fast(
    cotangent,
    courant_x,
    courant_y,
    diffusivity,
    vert_diff,
    level_count,
    edge_tile,
    edge_code,
    corner_tile,
    corner_code,
):
    levels, tracers, tiles_here, cells = cotangent.shape
    count = lax.axis_size("tile")
    reach = (2 * BAND + tiles_here - 1) // tiles_here
    vmem = pl.BlockSpec(memory_space=pltpu.VMEM)
    smem = pl.BlockSpec(memory_space=pltpu.SMEM)
    anywhere = pl.BlockSpec(memory_space=pl.ANY)
    base, strips = pl.pallas_call(
        solve_kernel,
        name="solve",
        out_shape=(
            jax.ShapeDtypeStruct((levels, 8, PADDED), jnp.float32),
            jax.ShapeDtypeStruct((levels, 8, 128), jnp.float32),
        ),
        in_specs=[smem] + [vmem] * 7,
        out_specs=(vmem, vmem),
        scratch_shapes=[
            pltpu.VMEM((levels, 8, cells), jnp.float32),
            pltpu.VMEM((levels, 8, cells), jnp.float32),
            pltpu.VMEM((8 * levels, PADDED + 128), jnp.float32),
        ],
        compiler_params=pltpu.CompilerParams(vmem_limit_bytes=40 << 20),
    )(edge_code, cotangent, courant_x, courant_y, diffusivity, vert_diff, level_count, strip_selector())
    near = pl.pallas_call(
        functools.partial(send_kernel, count, reach),
        name="send",
        out_shape=jax.ShapeDtypeStruct((2 * reach + 1, levels, 8, 128), jnp.float32),
        in_specs=[anywhere],
        out_specs=anywhere,
        scratch_shapes=[
            pltpu.SemaphoreType.DMA,
            pltpu.SemaphoreType.DMA((2 * reach + 1,)),
            pltpu.SemaphoreType.DMA((2 * reach + 1,)),
        ],
        compiler_params=pltpu.CompilerParams(collective_id=0, has_side_effects=True),
    )(strips)
    return pl.pallas_call(
        functools.partial(place_kernel, count, reach),
        name="place",
        out_shape=jax.ShapeDtypeStruct(cotangent.shape, jnp.float32),
        in_specs=[smem] * 4 + [vmem] * 4,
        out_specs=vmem,
        scratch_shapes=[pltpu.VMEM((8 * levels, 128), jnp.float32)],
        compiler_params=pltpu.CompilerParams(vmem_limit_bytes=40 << 20),
    )(edge_tile, edge_code, corner_tile, corner_code, near, base, level_count, strip_placer())


def solution(mesh):
    placed = (
        P("lev", None, "tile", None),
        P("lev", "tile", None),
        P("lev", "tile", None),
        P("tile", None),
        P("lev", "tile", None),
        P("tile", None),
        P("tile", None),
        P("tile", None),
        P("tile", None),
        P("tile", None),
    )
    fast = mesh.shape["lev"] == 1 and mesh.shape["tile"] > 2 * BAND
    return jax.shard_map(
        shards_fast if fast else shards, mesh=mesh, in_specs=placed, out_specs=P("lev", None, "tile", None), check_vma=False
    )
```

profile of v0, /device:TPU:0, one launch (start us, length us, event | category | flops | bytes accessed | tf_op | source)
XLA Modules:
  0.0 43.2 jit_solution(18363152352796674277)
XLA Ops:
  0.0 0.0 copy-start.1
  0.0 1.1 %copy-done.1 = f32[24,4,2,900]{3,2,1,0:T(2,128)S(1)} copy-done((f32[24,4,2,900]{3,2,1,0:T(2,128)S(1)}, f32[24,4,2,900]{3,2,1,0:T(2,128)}, u32[]{:S(2)}) %copy-start.1) | copy-done | bytes 691224
  1.1 0.0 copy-start.2
  1.1 1.1 %copy-done.2 = bf16[1152,256]{1,0:T(8,128)(2,1)S(1)} copy-done((bf16[1152,256]{1,0:T(8,128)(2,1)S(1)}, bf16[1152,256]{1,0:T(8,128)(2,1)}, u32[]{:S(2)}) %copy-start.2) | copy-done | bytes 589848
  2.2 0.0 copy-start.4
  2.2 0.9 %copy-done.4 = f32[24,2,900]{2,1,0:T(2,128)S(1)} copy-done((f32[24,2,900]{2,1,0:T(2,128)S(1)}, f32[24,2,900]{2,1,0:T(2,128)}, u32[]{:S(2)}) %copy-start.4) | copy-done | bytes 172824
  3.1 0.0 copy-start.5
  3.1 0.9 %copy-done.5 = f32[24,2,900]{2,1,0:T(2,128)S(1)} copy-done((f32[24,2,900]{2,1,0:T(2,128)S(1)}, f32[24,2,900]{2,1,0:T(2,128)}, u32[]{:S(2)}) %copy-start.5) | copy-done | bytes 172824
  4.1 0.0 copy-start.6
  4.1 0.9 %copy-done.6 = f32[24,2,900]{2,1,0:T(2,128)S(1)} copy-done((f32[24,2,900]{2,1,0:T(2,128)S(1)}, f32[24,2,900]{2,1,0:T(2,128)}, u32[]{:S(2)}) %copy-start.6) | copy-done | bytes 172824
  5.0 0.0 copy-start.8
  5.0 0.7 %copy-done.8 = s32[2,900]{1,0:T(2,128)S(1)} copy-done((s32[2,900]{1,0:T(2,128)S(1)}, s32[2,900]{1,0:T(2,128)}, u32[]{:S(2)}) %copy-start.8) | copy-done | bytes 7224
  5.7 0.0 copy-start.10
  5.7 0.7 %copy-done.10 = f32[2,900]{1,0:T(2,128)S(1)} copy-done((f32[2,900]{1,0:T(2,128)S(1)}, f32[2,900]{1,0:T(2,128)}, u32[]{:S(2)}) %copy-start.10) | copy-done | bytes 7224
  6.4 0.0 copy-start.11
  6.4 0.7 %copy-done.11 = s32[2,4]{1,0:T(2,128)S(1)} copy-done((s32[2,4]{1,0:T(2,128)S(1)}, s32[2,4]{1,0:T(2,128)}, u32[]{:S(2)}) %copy-start.11) | copy-done | bytes 56
  7.1 0.0 copy-start.3
  7.1 0.0 copy-start.9
  7.1 0.0 copy-start.12
  7.1 0.0 copy-start.13
  7.1 0.0 copy-start.14
  7.1 0.0 copy-start.15
  7.1 3.3 %solve.1 = (f32[24,8,1024]{2,1,0:T(8,128)S(1)}, f32[24,8,128]{2,1,0:T(8,128)S(1)}) custom-call(s32[2,4]{1,0:T(2,128)S(1)} %copy-done.11, f32[24,4,2,900]{3,2,1,0:T(2,128)S(1)} %copy-done.1, f32[24,2,900]{2,1,0:T(2,128)S(1)} %copy-done.4, f32[24,2,900]{2,1,0:T(2,128)S(1)} %copy-done.5, f32[2,900]{1,0:T(2,128)S(1)} %copy-done.10, f32[24,2,900]{2,1,0:T(2,128)S(1)} %copy-done.6, ...), custom_call_target="tpu_custom_call" | custom-call | tf_op jit(solution)/shard_map/solve/pallas_call | solution.py:425
  10.4 0.0 copy-start.7
  10.4 0.6 %copy-done.7 = f32[24,8,128]{2,1,0:T(8,128)} copy-done((f32[24,8,128]{2,1,0:T(8,128)}, f32[24,8,128]{2,1,0:T(8,128)S(1)}, u32[]{:S(2)}) %copy-start.7) | copy-done | bytes 98328
  11.0 28.3 %send.1.near_ref = f32[17,24,8,128]{3,2,1,0:T(8,128)} custom-call(f32[24,8,128]{2,1,0:T(8,128)} %copy-done.7), custom_call_target="tpu_custom_call" | custom-call | tf_op jit(solution)/shard_map/send/pallas_call | solution.py:441
  39.3 0.0 copy-done.3
  39.3 0.0 copy-done.9
  39.3 0.0 copy-done.12
  39.3 0.0 copy-done.13
  39.3 0.0 copy-done.14
  39.3 0.0 copy-done.15
  39.4 0.0 copy-start
  39.4 1.4 %copy-done = f32[17,24,8,128]{3,2,1,0:T(8,128)S(1)} copy-done((f32[17,24,8,128]{3,2,1,0:T(8,128)S(1)}, f32[17,24,8,128]{3,2,1,0:T(8,128)}, u32[]{:S(2)}) %copy-start) | copy-done | bytes 1671192
  40.8 2.4 %place.1 = f32[24,4,2,900]{3,2,1,0:T(2,128)} custom-call(s32[2,4]{1,0:T(2,128)S(1)} %copy-done.13, s32[2,4]{1,0:T(2,128)S(1)} %copy-done.12, s32[2,4]{1,0:T(2,128)S(1)} %copy-done.14, s32[2,4]{1,0:T(2,128)S(1)} %copy-done.15, f32[17,24,8,128]{3,2,1,0:T(8,128)S(1)} %copy-done, f32[24,8,1024]{2,1,0:T(8,128)S(1)} %get-tuple-element.8.base_ref, ...), custom_call_target="tpu_custom_call" | custom-call | tf_op jit(solution)/shard_map/place/pallas_call | solution.py:454
Async XLA Ops:
  0.0 1.1 %copy-start.1 = (f32[24,4,2,900]{3,2,1,0:T(2,128)S(1)}, f32[24,4,2,900]{3,2,1,0:T(2,128)}, u32[]{:S(2)}) copy-start(f32[24,4,2,900]{3,2,1,0:T(2,128)} %cot_ref.1) | copy-start | bytes 2073604
  1.1 1.1 %copy-start.2 = (bf16[1152,256]{1,0:T(8,128)(2,1)S(1)}, bf16[1152,256]{1,0:T(8,128)(2,1)}, u32[]{:S(2)}) copy-start(bf16[1152,256]{1,0:T(8,128)(2,1)} %constant.4.clone.sel_ref) | copy-start | bytes 1769476
  2.2 0.9 %copy-start.4 = (f32[24,2,900]{2,1,0:T(2,128)S(1)}, f32[24,2,900]{2,1,0:T(2,128)}, u32[]{:S(2)}) copy-start(f32[24,2,900]{2,1,0:T(2,128)} %cx_ref.1) | copy-start | bytes 518404
  3.1 0.9 %copy-start.5 = (f32[24,2,900]{2,1,0:T(2,128)S(1)}, f32[24,2,900]{2,1,0:T(2,128)}, u32[]{:S(2)}) copy-start(f32[24,2,900]{2,1,0:T(2,128)} %cy_ref.1) | copy-start | bytes 518404
  4.1 0.9 %copy-start.6 = (f32[24,2,900]{2,1,0:T(2,128)S(1)}, f32[24,2,900]{2,1,0:T(2,128)}, u32[]{:S(2)}) copy-start(f32[24,2,900]{2,1,0:T(2,128)} %vd_ref.1) | copy-start | bytes 518404
  5.0 0.7 %copy-start.8 = (s32[2,900]{1,0:T(2,128)S(1)}, s32[2,900]{1,0:T(2,128)}, u32[]{:S(2)}) copy-start(s32[2,900]{1,0:T(2,128)} %lc_ref.3) | copy-start | bytes 21604
  5.7 0.7 %copy-start.10 = (f32[2,900]{1,0:T(2,128)S(1)}, f32[2,900]{1,0:T(2,128)}, u32[]{:S(2)}) copy-start(f32[2,900]{1,0:T(2,128)} %dif_ref.1) | copy-start | bytes 21604
  6.4 0.7 %copy-start.11 = (s32[2,4]{1,0:T(2,128)S(1)}, s32[2,4]{1,0:T(2,128)}, u32[]{:S(2)}) copy-start(s32[2,4]{1,0:T(2,128)} %ec_ref.1) | copy-start | bytes 100
  7.1 32.2 %copy-start.3 = (bf16[128,1024]{1,0:T(8,128)(2,1)S(1)}, bf16[128,1024]{1,0:T(8,128)(2,1)}, u32[]{:S(2)}) copy-start(bf16[128,1024]{1,0:T(8,128)(2,1)} %constant.5.clone.place_ref) | copy-start | bytes 786436
  7.1 32.3 %copy-start.9 = (s32[2,900]{1,0:T(2,128)S(1)}, s32[2,900]{1,0:T(2,128)}, u32[]{:S(2)}) copy-start(s32[2,900]{1,0:T(2,128)} %lc_ref.3) | copy-start | bytes 21604
  7.1 32.3 %copy-start.12 = (s32[2,4]{1,0:T(2,128)S(1)}, s32[2,4]{1,0:T(2,128)}, u32[]{:S(2)}) copy-start(s32[2,4]{1,0:T(2,128)} %ec_ref.1) | copy-start | bytes 100
  7.1 32.3 %copy-start.13 = (s32[2,4]{1,0:T(2,128)S(1)}, s32[2,4]{1,0:T(2,128)}, u32[]{:S(2)}) copy-start(s32[2,4]{1,0:T(2,128)} %et_ref.1) | copy-start | bytes 100
  7.1 32.3 %copy-start.14 = (s32[2,4]{1,0:T(2,128)S(1)}, s32[2,4]{1,0:T(2,128)}, u32[]{:S(2)}) copy-start(s32[2,4]{1,0:T(2,128)} %ct_ref.1) | copy-start | bytes 100
  7.1 32.3 %copy-start.15 = (s32[2,4]{1,0:T(2,128)S(1)}, s32[2,4]{1,0:T(2,128)}, u32[]{:S(2)}) copy-start(s32[2,4]{1,0:T(2,128)} %cc_ref.1) | copy-start | bytes 100
  10.4 0.6 %copy-start.7 = (f32[24,8,128]{2,1,0:T(8,128)}, f32[24,8,128]{2,1,0:T(8,128)S(1)}, u32[]{:S(2)}) copy-start(f32[24,8,128]{2,1,0:T(8,128)S(1)} %get-tuple-element.7.strips_ref) | copy-start | bytes 294916
  39.4 1.4 %copy-start = (f32[17,24,8,128]{3,2,1,0:T(8,128)S(1)}, f32[17,24,8,128]{3,2,1,0:T(8,128)}, u32[]{:S(2)}) copy-start(f32[17,24,8,128]{3,2,1,0:T(8,128)} %send.1.near_ref) | copy-start | bytes 5013508
where the time goes:
time: 43.6 us; the launch traced here: 43.2 us
  Pallas kernels  33.9 us (78%)
  local copies, waits for them, and re-layouts  9.14 us (21%)
    pallas_call x1, Pallas kernels, shards_fast(): pl.pallas_call(functools.partial(send_kernel, count, reach), name='send',...  28.3 us
    unnamed x32, local copies, waits for them, and re-layouts  9.14 us
    pallas_call x1, Pallas kernels, shards_fast(): pl.pallas_call(solve_kernel, name='solve', out_shape=(jax.ShapeDtypeStruc...  3.26 us
    pallas_call x1, Pallas kernels, shards_fast(): pl.pallas_call(functools.partial(place_kernel, count, reach), name='place...  2.39 us

commit v1 on v0

--- a/solution.py
+++ b/solution.py
@@ -217,6 +217,7 @@
 
 PADDED = 1024
 SIDE_LANES = 32
+PLANE = 4
 MESH = pl.DeviceIdType.MESH
 
 
@@ -260,11 +261,30 @@
 
 
 def solve_kernel(
-    code_ref, cot_ref, cx_ref, cy_ref, dif_ref, vd_ref, lc_ref, sel_ref,
+    code_hbm, cot_hbm, cx_hbm, cy_hbm, dif_hbm, vd_hbm, lc_hbm, sel_hbm,
     base_ref, strips_ref, factor_ref, partial_ref, edge_ref,
+    code_ref, cot_ref, cx_ref, cy_ref, dif_ref, vd_ref, lc_ref, sel_ref, sems,
 ):
     levels = cot_ref.shape[0]
     cells = cot_ref.shape[3]
+    pairs = [
+        (lc_hbm, lc_ref),
+        (vd_hbm, vd_ref),
+        (cot_hbm, cot_ref),
+        (dif_hbm, dif_ref),
+        (cx_hbm, cx_ref),
+        (cy_hbm, cy_ref),
+        (code_hbm, code_ref),
+        (sel_hbm, sel_ref),
+    ]
+    copies = [
+        pltpu.make_async_copy(source, target, sems.at[i])
+        for i, (source, target) in enumerate(pairs)
+    ]
+    for copy in copies:
+        copy.start()
+    for copy in copies[:3]:
+        copy.wait()
     depth = four_times(lc_ref[...])
 
     def coupling(k):
@@ -295,6 +315,8 @@
     corner_0 = (short == 0) | (short == EDGE - 1)
     corner_6 = short == ((EDGE - 1) * EDGE) % 128
     corner_7 = short == (EDGE * EDGE - 1) % 128
+    for copy in copies[3:6]:
+        copy.wait()
     diffuse = widen(four_times(dif_ref[...]))
     quarter = 0.25 * diffuse
     centre = 1.0 - 5.0 * diffuse
@@ -322,6 +344,8 @@
             + jnp.where(corner_6, diagonal[:, 768:896], 0.0)
             + jnp.where(corner_7, diagonal[:, 896:1024], 0.0)
         )
+    for copy in copies[6:]:
+        copy.wait()
     both_ways = split_dot(edge_ref[...], sel_ref[...])
     parity = lax.rem(lax.broadcasted_iota(jnp.int32, (8, 128), 0), 2)
     code = jnp.zeros((8, 128), jnp.int32)
@@ -334,36 +358,83 @@
         strips_ref[k] = jnp.where(flipped, rows[:, 128:], rows[:, :128])
 
 
-def send_kernel(count, reach, strips_ref, near_ref, own_sem, send_sem, recv_sem):
+def send_kernel(count, strips_ref, near_ref, own_sem, send_sem, recv_sem):
+    chips = count // 2
     me = lax.axis_index("tile")
+    chip = me // 2
+    core = lax.rem(me, 2)
+    place = lax.rem(chip, PLANE)
+
+    def at(steps):
+        return 2 * lax.rem(chip + steps + chips, chips) + core
+
+    partner = me + 1 - 2 * core
+    wraps = [(place + j) // PLANE for j in range(PLANE)]
+    beside = [at(j - PLANE * wraps[j]) for j in range(PLANE)]
+    above, below = at(PLANE), at(-PLANE)
     barrier = pltpu.get_barrier_semaphore()
-    offsets = [o for o in range(-reach, reach + 1) if o != 0]
-    for o in offsets:
-        pl.semaphore_signal(
-            barrier, inc=1, device_id={"tile": lax.rem(me + o + count, count)}, device_id_type=MESH
-        )
-    own = pltpu.make_async_copy(strips_ref, near_ref.at[reach], own_sem)
+    peers = [partner, above, below] + beside[1:]
+    for peer in peers:
+        pl.semaphore_signal(barrier, inc=1, device_id={"tile": peer}, device_id_type=MESH)
+    own = pltpu.make_async_copy(strips_ref, near_ref.at[PLANE, core], own_sem)
     own.start()
-    pl.semaphore_wait(barrier, len(offsets))
+    pl.semaphore_wait(barrier, len(peers))
     copies = []
-    for o in offsets:
+
+    def send(source, spot, to):
         copy = pltpu.make_async_remote_copy(
-            src_ref=strips_ref,
-            dst_ref=near_ref.at[reach - o],
-            send_sem=send_sem.at[reach + o],
-            recv_sem=recv_sem.at[reach - o],
-            device_id={"tile": lax.rem(me + o + count, count)},
+            src_ref=source,
+            dst_ref=near_ref.at[spot, core],
+            send_sem=send_sem.at[len(copies)],
+            recv_sem=recv_sem.at[spot, core],
+            device_id={"tile": to},
             device_id_type=MESH,
         )
         copy.start()
         copies.append(copy)
+
+    def arrived(spot, side):
+        pltpu.make_async_remote_copy(
+            src_ref=strips_ref,
+            dst_ref=near_ref.at[spot, side],
+            send_sem=own_sem,
+            recv_sem=recv_sem.at[spot, side],
+            device_id={"tile": partner},
+            device_id_type=MESH,
+        ).wait_recv()
+
+    def share(spot):
+        send(near_ref.at[spot, core], spot, partner)
+
+    send(strips_ref, 0, above)
+    send(strips_ref, 2 * PLANE, below)
+    for j in range(1, PLANE):
+        send(strips_ref, PLANE - j + PLANE * wraps[j], beside[j])
+    send(strips_ref, PLANE, partner)
+    arrived(0, core)
+    arrived(2 * PLANE, core)
+    for j in range(1, PLANE):
+        source = near_ref.at[2 * PLANE - 2 * PLANE * wraps[j], core]
+        send(source, 2 * PLANE - PLANE * wraps[j] - j, beside[j])
+    share(0)
+    share(2 * PLANE)
+    for j in range(1, PLANE):
+        spot = PLANE + j - PLANE * wraps[j]
+        arrived(spot, core)
+        share(spot)
+    for j in range(1, PLANE):
+        spot = j + PLANE * wraps[j]
+        arrived(spot, core)
+        share(spot)
+    for spot in range(2 * PLANE + 1):
+        arrived(spot, 1 - core)
     own.wait()
     for copy in copies:
-        copy.wait()
+        copy.wait_send()
 
 
 def place_kernel(
-    count, reach, et_ref, ec_ref, ct_ref, cc_ref, near_ref, base_ref, lc_ref, place_ref,
+    count, et_ref, ec_ref, ct_ref, cc_ref, near_ref, base_ref, lc_ref, place_ref,
     out_ref, arriving_ref,
 ):
     levels = base_ref.shape[0]
@@ -382,9 +453,9 @@
             for side in range(4):
                 tile = tiles_ref[i, side]
                 there = jnp.maximum(tile, 0)
-                slot = lax.rem(there // 2 - me + reach + count, count)
+                slot = lax.rem(there // 4 - me // 2 + PLANE + count // 2, count // 2)
                 slot = jnp.where(tile < 0, 0, slot)
-                values = near_ref[slot]
+                values = near_ref[slot, lax.rem(there // 2, 2)]
                 values = jnp.where(
                     lax.rem(there, 2) == i, values, pltpu.roll(values, 1 if i == 1 else 7, 1)
                 )
@@ -418,10 +489,9 @@
 ):
     levels, tracers, tiles_here, cells = cotangent.shape
     count = lax.axis_size("tile")
-    reach = (2 * BAND + tiles_here - 1) // tiles_here
     vmem = pl.BlockSpec(memory_space=pltpu.VMEM)
     smem = pl.BlockSpec(memory_space=pltpu.SMEM)
-    anywhere = pl.BlockSpec(memory_space=pl.ANY)
+    hbm = pl.BlockSpec(memory_space=pltpu.HBM)
     base, strips = pl.pallas_call(
         solve_kernel,
         name="solve",
@@ -429,30 +499,39 @@
             jax.ShapeDtypeStruct((levels, 8, PADDED), jnp.float32),
             jax.ShapeDtypeStruct((levels, 8, 128), jnp.float32),
         ),
-        in_specs=[smem] + [vmem] * 7,
+        in_specs=[hbm] * 8,
         out_specs=(vmem, vmem),
         scratch_shapes=[
             pltpu.VMEM((levels, 8, cells), jnp.float32),
             pltpu.VMEM((levels, 8, cells), jnp.float32),
             pltpu.VMEM((8 * levels, PADDED + 128), jnp.float32),
+            pltpu.SMEM(edge_code.shape, jnp.int32),
+            pltpu.VMEM(cotangent.shape, jnp.float32),
+            pltpu.VMEM(courant_x.shape, jnp.float32),
+            pltpu.VMEM(courant_y.shape, jnp.float32),
+            pltpu.VMEM(diffusivity.shape, jnp.float32),
+            pltpu.VMEM(vert_diff.shape, jnp.float32),
+            pltpu.VMEM(level_count.shape, jnp.int32),
+            pltpu.VMEM((PADDED + 128, 256), jnp.bfloat16),
+            pltpu.SemaphoreType.DMA((8,)),
         ],
-        compiler_params=pltpu.CompilerParams(vmem_limit_bytes=40 << 20),
+        compiler_params=pltpu.CompilerParams(vmem_limit_bytes=62 << 20),
     )(edge_code, cotangent, courant_x, courant_y, diffusivity, vert_diff, level_count, strip_selector())
     near = pl.pallas_call(
-        functools.partial(send_kernel, count, reach),
+        functools.partial(send_kernel, count),
         name="send",
-        out_shape=jax.ShapeDtypeStruct((2 * reach + 1, levels, 8, 128), jnp.float32),
-        in_specs=[anywhere],
-        out_specs=anywhere,
+        out_shape=jax.ShapeDtypeStruct((2 * PLANE + 1, 2, levels, 8, 128), jnp.float32),
+        in_specs=[hbm],
+        out_specs=hbm,
         scratch_shapes=[
             pltpu.SemaphoreType.DMA,
-            pltpu.SemaphoreType.DMA((2 * reach + 1,)),
-            pltpu.SemaphoreType.DMA((2 * reach + 1,)),
+            pltpu.SemaphoreType.DMA((4 * PLANE + 1,)),
+            pltpu.SemaphoreType.DMA((2 * PLANE + 1, 2)),
         ],
         compiler_params=pltpu.CompilerParams(collective_id=0, has_side_effects=True),
     )(strips)
     return pl.pallas_call(
-        functools.partial(place_kernel, count, reach),
+        functools.partial(place_kernel, count),
         name="place",
         out_shape=jax.ShapeDtypeStruct(cotangent.shape, jnp.float32),
         in_specs=[smem] * 4 + [vmem] * 4,
@@ -475,7 +554,7 @@
         P("tile", None),
         P("tile", None),
     )
-    fast = mesh.shape["lev"] == 1 and mesh.shape["tile"] > 2 * BAND
+    fast = mesh.shape["lev"] == 1 and mesh.shape["tile"] % 8 == 0 and mesh.shape["tile"] > 2 * BAND
     return jax.shard_map(
         shards_fast if fast else shards, mesh=mesh, in_specs=placed, out_specs=P("lev", None, "tile", None), check_vma=False
     )

time: 43.6 us -> 27.5 us (0.63)
  Pallas kernels: 33.9 us -> 25.7 us
  local copies, waits for them, and re-layouts: 9.14 us -> 1.5 us
    pallas_call x2, Pallas kernels: 30.7 us -> 20.4 us  [the longest x1 17.9 us: shards_fast(): pl.pallas_call(functools.partial(send_kernel, count), name='send', out_sh...]
    unnamed x32 -> x16, local copies, waits for them, and re-layouts: 9.14 us -> 1.5 us
    pallas_call x1, Pallas kernels: 3.26 us -> 5.37 us  [shards_fast(): pl.pallas_call(solve_kernel, name='solve', out_shape=(jax.ShapeDtypeStruc...]
where the time goes in v1:
time: 27.5 us; the launch traced here: 27.3 us
  Pallas kernels  25.7 us (93%)
  local copies, waits for them, and re-layouts  1.5 us (5%)
    pallas_call x1, Pallas kernels, shards_fast(): pl.pallas_call(functools.partial(send_kernel, count), name='send', out_sh...  17.9 us
    pallas_call x1, Pallas kernels, shards_fast(): pl.pallas_call(solve_kernel, name='solve', out_shape=(jax.ShapeDtypeStruc...  5.37 us
    pallas_call x1, Pallas kernels, shards_fast(): pl.pallas_call(functools.partial(place_kernel, count), name='place', out_...  2.46 us
    unnamed x16, local copies, waits for them, and re-layouts  1.5 us

profile of v1, /device:TPU:0, one launch (start us, length us, event | category | flops | bytes accessed | tf_op | source)
XLA Modules:
  0.0 27.3 jit_solution(8333637953426550272)
XLA Ops:
  0.0 0.0 copy-start.2
  0.0 0.0 copy-start.4
  0.0 0.0 copy-start.3
  0.0 0.0 copy-start.7
  0.0 0.0 copy-start.6
  0.0 0.0 copy-start.5
  0.0 5.4 %solve.1 = (f32[24,8,1024]{2,1,0:T(8,128)}, f32[24,8,128]{2,1,0:T(8,128)}) custom-call(s32[2,4]{1,0:T(2,128)} %ec_ref.1, f32[24,4,2,900]{3,2,1,0:T(2,128)} %cot_hbm.1, f32[24,2,900]{2,1,0:T(2,128)} %cx_hbm.1, f32[24,2,900]{2,1,0:T(2,128)} %cy_hbm.1, f32[2,900]{1,0:T(2,128)} %dif_hbm.1, f32[24,2,900]{2,1,0:T(2,128)} %vd_hbm.1, s32[2,900]{1,0:T(2,128)} %lc_ref.1, ...), custom_call_target="tpu_custom_call" | custom-call | tf_op jit(solution)/shard_map/solve/pallas_call | solution.py:495
  5.4 0.0 copy-start.1
  5.4 17.9 %send.1.near_ref = f32[9,2,24,8,128]{4,3,2,1,0:T(8,128)} custom-call(f32[24,8,128]{2,1,0:T(8,128)} %get-tuple-element.7.strips_ref), custom_call_target="tpu_custom_call" | custom-call | tf_op jit(solution)/shard_map/send/pallas_call | solution.py:520
  23.3 0.0 copy-done.2
  23.3 0.0 copy-done.4
  23.3 0.0 copy-done.3
  23.3 0.0 copy-done.7
  23.4 0.0 copy-done.6
  23.4 0.0 copy-done.5
  23.4 0.0 copy-done.1
  23.4 0.0 copy-start
  23.4 1.5 %copy-done = f32[9,2,24,8,128]{4,3,2,1,0:T(8,128)S(1)} copy-done((f32[9,2,24,8,128]{4,3,2,1,0:T(8,128)S(1)}, f32[9,2,24,8,128]{4,3,2,1,0:T(8,128)}, u32[]{:S(2)}) %copy-start) | copy-done | bytes 1769496
  24.9 2.5 %place.1 = f32[24,4,2,900]{3,2,1,0:T(2,128)} custom-call(s32[2,4]{1,0:T(2,128)S(1)} %copy-done.5, s32[2,4]{1,0:T(2,128)S(1)} %copy-done.4, s32[2,4]{1,0:T(2,128)S(1)} %copy-done.6, s32[2,4]{1,0:T(2,128)S(1)} %copy-done.7, f32[9,2,24,8,128]{4,3,2,1,0:T(8,128)S(1)} %copy-done, f32[24,8,1024]{2,1,0:T(8,128)S(1)} %copy-done.1, s32[2,900]{1,0:T(2,128)S(1)} %copy-done.3, ...), custom_call_target="tpu_custom_call" | custom-call | tf_op jit(solution)/shard_map/place/pallas_call | solution.py:533
Async XLA Ops:
  0.0 23.3 %copy-start.2 = (bf16[128,1024]{1,0:T(8,128)(2,1)S(1)}, bf16[128,1024]{1,0:T(8,128)(2,1)}, u32[]{:S(2)}) copy-start(bf16[128,1024]{1,0:T(8,128)(2,1)} %constant.5.clone.place_ref) | copy-start | bytes 786436
  0.0 23.3 %copy-start.4 = (s32[2,4]{1,0:T(2,128)S(1)}, s32[2,4]{1,0:T(2,128)}, u32[]{:S(2)}) copy-start(s32[2,4]{1,0:T(2,128)} %ec_ref.1) | copy-start | bytes 100
  0.0 23.3 %copy-start.3 = (s32[2,900]{1,0:T(2,128)S(1)}, s32[2,900]{1,0:T(2,128)}, u32[]{:S(2)}) copy-start(s32[2,900]{1,0:T(2,128)} %lc_ref.1) | copy-start | bytes 21604
  0.0 23.3 %copy-start.7 = (s32[2,4]{1,0:T(2,128)S(1)}, s32[2,4]{1,0:T(2,128)}, u32[]{:S(2)}) copy-start(s32[2,4]{1,0:T(2,128)} %cc_ref.1) | copy-start | bytes 100
  0.0 23.3 %copy-start.6 = (s32[2,4]{1,0:T(2,128)S(1)}, s32[2,4]{1,0:T(2,128)}, u32[]{:S(2)}) copy-start(s32[2,4]{1,0:T(2,128)} %ct_ref.1) | copy-start | bytes 100
  0.0 23.4 %copy-start.5 = (s32[2,4]{1,0:T(2,128)S(1)}, s32[2,4]{1,0:T(2,128)}, u32[]{:S(2)}) copy-start(s32[2,4]{1,0:T(2,128)} %et_ref.1) | copy-start | bytes 100
  5.4 18.0 %copy-start.1 = (f32[24,8,1024]{2,1,0:T(8,128)S(1)}, f32[24,8,1024]{2,1,0:T(8,128)}, u32[]{:S(2)}) copy-start(f32[24,8,1024]{2,1,0:T(8,128)} %get-tuple-element.8.base_ref) | copy-start | bytes 2359300
  23.4 1.5 %copy-start = (f32[9,2,24,8,128]{4,3,2,1,0:T(8,128)S(1)}, f32[9,2,24,8,128]{4,3,2,1,0:T(8,128)}, u32[]{:S(2)}) copy-start(f32[9,2,24,8,128]{4,3,2,1,0:T(8,128)} %send.1.near_ref) | copy-start | bytes 5308420

commit v2 on v1

--- a/solution.py
+++ b/solution.py
@@ -218,6 +218,7 @@
 PADDED = 1024
 SIDE_LANES = 32
 PLANE = 4
+CHUNKS = 4
 MESH = pl.DeviceIdType.MESH
 
 
@@ -262,7 +263,7 @@
 
 def solve_kernel(
     code_hbm, cot_hbm, cx_hbm, cy_hbm, dif_hbm, vd_hbm, lc_hbm, sel_hbm,
-    base_ref, strips_ref, factor_ref, partial_ref, edge_ref,
+    base_hbm, strips_ref, base_ref, factor_ref, partial_ref, edge_ref,
     code_ref, cot_ref, cx_ref, cy_ref, dif_ref, vd_ref, lc_ref, sel_ref, sems,
 ):
     levels = cot_ref.shape[0]
@@ -270,7 +271,6 @@
     pairs = [
         (lc_hbm, lc_ref),
         (vd_hbm, vd_ref),
-        (cot_hbm, cot_ref),
         (dif_hbm, dif_ref),
         (cx_hbm, cx_ref),
         (cy_hbm, cy_ref),
@@ -281,9 +281,26 @@
         pltpu.make_async_copy(source, target, sems.at[i])
         for i, (source, target) in enumerate(pairs)
     ]
-    for copy in copies:
+    chunk = levels // CHUNKS
+    arrivals = [
+        pltpu.make_async_copy(
+            cot_hbm.at[c * chunk : (c + 1) * chunk],
+            cot_ref.at[c * chunk : (c + 1) * chunk],
+            sems.at[len(pairs) + c],
+        )
+        for c in range(CHUNKS)
+    ]
+    leaving = [
+        pltpu.make_async_copy(
+            base_ref.at[c * chunk : (c + 1) * chunk],
+            base_hbm.at[c * chunk : (c + 1) * chunk],
+            sems.at[len(pairs) + CHUNKS + c],
+        )
+        for c in range(CHUNKS)
+    ]
+    for copy in copies[:2] + arrivals + copies[2:]:
         copy.start()
-    for copy in copies[:3]:
+    for copy in copies[:2]:
         copy.wait()
     depth = four_times(lc_ref[...])
 
@@ -296,6 +313,8 @@
     partial_value = jnp.zeros((8, cells), jnp.float32)
     upper = coupling(0)
     for k in range(levels):
+        if k % chunk == 0:
+            arrivals[k // chunk].wait()
         lower = coupling(k + 1)
         source = jnp.concatenate([cot_ref[k, n] for n in range(4)], axis=0)
         inverse = 1.0 / ((1.0 + upper + lower) + upper * factor)
@@ -315,7 +334,7 @@
     corner_0 = (short == 0) | (short == EDGE - 1)
     corner_6 = short == ((EDGE - 1) * EDGE) % 128
     corner_7 = short == (EDGE * EDGE - 1) % 128
-    for copy in copies[3:6]:
+    for copy in copies[2:5]:
         copy.wait()
     diffuse = widen(four_times(dif_ref[...]))
     quarter = 0.25 * diffuse
@@ -344,7 +363,9 @@
             + jnp.where(corner_6, diagonal[:, 768:896], 0.0)
             + jnp.where(corner_7, diagonal[:, 896:1024], 0.0)
         )
-    for copy in copies[6:]:
+        if k % chunk == 0:
+            leaving[k // chunk].start()
+    for copy in copies[5:]:
         copy.wait()
     both_ways = split_dot(edge_ref[...], sel_ref[...])
     parity = lax.rem(lax.broadcasted_iota(jnp.int32, (8, 128), 0), 2)
@@ -356,6 +377,8 @@
     for k in range(levels):
         rows = both_ways[8 * k : 8 * k + 8]
         strips_ref[k] = jnp.where(flipped, rows[:, 128:], rows[:, :128])
+    for copy in leaving:
+        copy.wait()
 
 
 def send_kernel(count, strips_ref, near_ref, own_sem, send_sem, recv_sem):
@@ -434,45 +457,91 @@
 
 
 def place_kernel(
-    count, et_ref, ec_ref, ct_ref, cc_ref, near_ref, base_ref, lc_ref, place_ref,
-    out_ref, arriving_ref,
+    count, et_hbm, ec_hbm, ct_hbm, cc_hbm, near_hbm, base_hbm, lc_hbm, place_hbm,
+    out_hbm, et_ref, ec_ref, ct_ref, cc_ref, base_ref, lc_ref, place_ref, block_ref,
+    arriving_ref, out_ref, sems, block_sems, out_sems,
 ):
     levels = base_ref.shape[0]
     cells = out_ref.shape[3]
     me = lax.axis_index("tile")
+    pairs = [
+        (et_hbm, et_ref),
+        (ec_hbm, ec_ref),
+        (ct_hbm, ct_ref),
+        (cc_hbm, cc_ref),
+        (place_hbm, place_ref),
+        (lc_hbm, lc_ref),
+        (base_hbm, base_ref),
+    ]
+    copies = [
+        pltpu.make_async_copy(source, target, sems.at[i])
+        for i, (source, target) in enumerate(pairs)
+    ]
+    for copy in copies[:4]:
+        copy.start()
     lane = lax.broadcasted_iota(jnp.int32, (8, 128), 1)
     parity = lax.rem(lax.broadcasted_iota(jnp.int32, (8, 128), 0), 2)
     group = lane // SIDE_LANES
     spot = lax.rem(lane, SIDE_LANES)
-    total = jnp.zeros((levels, 8, 128), jnp.float32)
-    for i in range(2):
+    for copy in copies[:4]:
+        copy.wait()
+    units = [
+        (i, side, tiles_ref, codes_ref, wanted)
         for tiles_ref, codes_ref, wanted in (
             (et_ref, ec_ref, spot < EDGE),
             (ct_ref, cc_ref, spot == EDGE),
-        ):
-            for side in range(4):
-                tile = tiles_ref[i, side]
-                there = jnp.maximum(tile, 0)
-                slot = lax.rem(there // 4 - me // 2 + PLANE + count // 2, count // 2)
-                slot = jnp.where(tile < 0, 0, slot)
-                values = near_ref[slot, lax.rem(there // 2, 2)]
-                values = jnp.where(
-                    lax.rem(there, 2) == i, values, pltpu.roll(values, 1 if i == 1 else 7, 1)
-                )
-                shift = lax.rem(SIDE_LANES * (side - lax.rem(codes_ref[i, side], 4)) + 128, 128)
-                values = pltpu.roll(values, shift, 2)
-                chosen = wanted & (group == side) & (parity == i) & (tile >= 0)
-                total = jnp.where(chosen[None], values, total)
+        )
+        for i in range(2)
+        for side in range(4)
+    ]
+    blocks = []
+    for index, (i, side, tiles_ref, codes_ref, wanted) in enumerate(units):
+        tile = tiles_ref[i, side]
+        there = jnp.maximum(tile, 0)
+        slot = lax.rem(there // 4 - me // 2 + PLANE + count // 2, count // 2)
+        slot = jnp.where(tile < 0, PLANE, slot)
+        block = pltpu.make_async_copy(
+            near_hbm.at[slot, lax.rem(there // 2, 2)], block_ref.at[index], block_sems.at[index]
+        )
+        block.start()
+        blocks.append(block)
+    for copy in copies[4:]:
+        copy.start()
+    total = jnp.zeros((levels, 8, 128), jnp.float32)
+    for index, (i, side, tiles_ref, codes_ref, wanted) in enumerate(units):
+        tile = tiles_ref[i, side]
+        there = jnp.maximum(tile, 0)
+        blocks[index].wait()
+        values = block_ref[index]
+        values = jnp.where(
+            lax.rem(there, 2) == i, values, pltpu.roll(values, 1 if i == 1 else 7, 1)
+        )
+        shift = lax.rem(SIDE_LANES * (side - lax.rem(codes_ref[i, side], 4)) + 128, 128)
+        values = pltpu.roll(values, shift, 2)
+        chosen = wanted & (group == side) & (parity == i) & (tile >= 0)
+        total = jnp.where(chosen[None], values, total)
     for k in range(levels):
         arriving_ref[8 * k : 8 * k + 8] = total[k]
-    returned = split_dot(arriving_ref[...], place_ref[...])
+    for copy in copies[4:]:
+        copy.wait()
     depth = four_times(lc_ref[...])
-    for k in range(levels):
-        result = base_ref[k][:, :cells] + jnp.where(
-            k < depth, returned[8 * k : 8 * k + 8, :cells], 0.0
-        )
-        for n in range(4):
-            out_ref[k, n] = result[2 * n : 2 * n + 2]
+    chunk = levels // CHUNKS
+    leaving = []
+    for c in range(CHUNKS):
+        here = slice(c * chunk, (c + 1) * chunk)
+        returned = split_dot(arriving_ref[8 * c * chunk : 8 * (c + 1) * chunk], place_ref[...])
+        for k in range(c * chunk, (c + 1) * chunk):
+            row = 8 * (k - c * chunk)
+            result = base_ref[k][:, :cells] + jnp.where(
+                k < depth, returned[row : row + 8, :cells], 0.0
+            )
+            for n in range(4):
+                out_ref[k, n] = result[2 * n : 2 * n + 2]
+        copy = pltpu.make_async_copy(out_ref.at[here], out_hbm.at[here], out_sems.at[c])
+        copy.start()
+        leaving.append(copy)
+    for copy in leaving:
+        copy.wait()
 
 
 def shards_fast(
@@ -490,7 +559,6 @@
     levels, tracers, tiles_here, cells = cotangent.shape
     count = lax.axis_size("tile")
     vmem = pl.BlockSpec(memory_space=pltpu.VMEM)
-    smem = pl.BlockSpec(memory_space=pltpu.SMEM)
     hbm = pl.BlockSpec(memory_space=pltpu.HBM)
     base, strips = pl.pallas_call(
         solve_kernel,
@@ -500,8 +568,9 @@
             jax.ShapeDtypeStruct((levels, 8, 128), jnp.float32),
         ),
         in_specs=[hbm] * 8,
-        out_specs=(vmem, vmem),
+        out_specs=(hbm, vmem),
         scratch_shapes=[
+            pltpu.VMEM((levels, 8, PADDED), jnp.float32),
             pltpu.VMEM((levels, 8, cells), jnp.float32),
             pltpu.VMEM((levels, 8, cells), jnp.float32),
             pltpu.VMEM((8 * levels, PADDED + 128), jnp.float32),
@@ -513,7 +582,7 @@
             pltpu.VMEM(vert_diff.shape, jnp.float32),
             pltpu.VMEM(level_count.shape, jnp.int32),
             pltpu.VMEM((PADDED + 128, 256), jnp.bfloat16),
-            pltpu.SemaphoreType.DMA((8,)),
+            pltpu.SemaphoreType.DMA((7 + 2 * CHUNKS,)),
         ],
         compiler_params=pltpu.CompilerParams(vmem_limit_bytes=62 << 20),
     )(edge_code, cotangent, courant_x, courant_y, diffusivity, vert_diff, level_count, strip_selector())
@@ -534,10 +603,21 @@
         functools.partial(place_kernel, count),
         name="place",
         out_shape=jax.ShapeDtypeStruct(cotangent.shape, jnp.float32),
-        in_specs=[smem] * 4 + [vmem] * 4,
-        out_specs=vmem,
-        scratch_shapes=[pltpu.VMEM((8 * levels, 128), jnp.float32)],
-        compiler_params=pltpu.CompilerParams(vmem_limit_bytes=40 << 20),
+        in_specs=[hbm] * 8,
+        out_specs=hbm,
+        scratch_shapes=[pltpu.SMEM(edge_tile.shape, jnp.int32)] * 4
+        + [
+            pltpu.VMEM((levels, 8, PADDED), jnp.float32),
+            pltpu.VMEM(level_count.shape, jnp.int32),
+            pltpu.VMEM((128, PADDED), jnp.bfloat16),
+            pltpu.VMEM((16, levels, 8, 128), jnp.float32),
+            pltpu.VMEM((8 * levels, 128), jnp.float32),
+            pltpu.VMEM(cotangent.shape, jnp.float32),
+            pltpu.SemaphoreType.DMA((7,)),
+            pltpu.SemaphoreType.DMA((16,)),
+            pltpu.SemaphoreType.DMA((CHUNKS,)),
+        ],
+        compiler_params=pltpu.CompilerParams(vmem_limit_bytes=62 << 20),
     )(edge_tile, edge_code, corner_tile, corner_code, near, base, level_count, strip_placer())
 
 

time: 27.5 us -> 28.2 us (1.025)
  Pallas kernels: 25.7 us -> 27.9 us
  local copies, waits for them, and re-layouts: 1.5 us -> 0 us
    pallas_call x1, Pallas kernels: 2.46 us -> 4.6 us  [shards_fast(): pl.pallas_call(functools.partial(place_kernel, count), name='place', out_...]
    unnamed x16 -> x0, local copies, waits for them, and re-layouts: 1.5 us -> none
where the time goes in v2:
time: 28.2 us; the launch traced here: 27.9 us
  Pallas kernels  27.9 us (99%)
    pallas_call x1, Pallas kernels, shards_fast(): pl.pallas_call(functools.partial(send_kernel, count), name='send', out_sh...  17.9 us
    pallas_call x1, Pallas kernels, shards_fast(): pl.pallas_call(solve_kernel, name='solve', out_shape=(jax.ShapeDtypeStruc...  5.43 us
    pallas_call x1, Pallas kernels, shards_fast(): pl.pallas_call(functools.partial(place_kernel, count), name='place', out_...  4.6 us

profile of v2, /device:TPU:0, one launch (start us, length us, event | category | flops | bytes accessed | tf_op | source)
XLA Modules:
  0.0 27.9 jit_solution(14115593071553988045)
XLA Ops:
  0.0 5.4 %solve.1 = (f32[24,8,1024]{2,1,0:T(8,128)}, f32[24,8,128]{2,1,0:T(8,128)}) custom-call(s32[2,4]{1,0:T(2,128)} %ec_hbm.1, f32[24,4,2,900]{3,2,1,0:T(2,128)} %cot_hbm.1, f32[24,2,900]{2,1,0:T(2,128)} %cx_hbm.1, f32[24,2,900]{2,1,0:T(2,128)} %cy_hbm.1, f32[2,900]{1,0:T(2,128)} %dif_hbm.1, f32[24,2,900]{2,1,0:T(2,128)} %vd_hbm.1, s32[2,900]{1,0:T(2,128)} %lc_hbm.3, ...), custom_call_target="tpu_custom_call" | custom-call | tf_op jit(solution)/shard_map/solve/pallas_call | solution.py:563
  5.4 17.9 %send.1.near_hbm = f32[9,2,24,8,128]{4,3,2,1,0:T(8,128)} custom-call(f32[24,8,128]{2,1,0:T(8,128)} %get-tuple-element.7.strips_ref), custom_call_target="tpu_custom_call" | custom-call | tf_op jit(solution)/shard_map/send/pallas_call | solution.py:589
  23.3 4.6 %place.1 = f32[24,4,2,900]{3,2,1,0:T(2,128)} custom-call(s32[2,4]{1,0:T(2,128)} %et_hbm.1, s32[2,4]{1,0:T(2,128)} %ec_hbm.1, s32[2,4]{1,0:T(2,128)} %ct_hbm.1, s32[2,4]{1,0:T(2,128)} %cc_hbm.1, f32[9,2,24,8,128]{4,3,2,1,0:T(8,128)} %send.1.near_hbm, f32[24,8,1024]{2,1,0:T(8,128)} %get-tuple-element.8.base_hbm, s32[2,900]{1,0:T(2,128)} %lc_hbm.3, ...), custom_call_target="tpu_custom_call" | custom-call | tf_op jit(solution)/shard_map/place/pallas_call | solution.py:602

commit v3 on v1

--- a/solution.py
+++ b/solution.py
@@ -218,6 +218,7 @@
 PADDED = 1024
 SIDE_LANES = 32
 PLANE = 4
+HALVES = 2
 MESH = pl.DeviceIdType.MESH
 
 
@@ -380,54 +381,67 @@
     own.start()
     pl.semaphore_wait(barrier, len(peers))
     copies = []
-
-    def send(source, spot, to):
+    size = strips_ref.shape[0] // HALVES
+
+    def part(spot, side, half):
+        return near_ref.at[spot, side, half * size : (half + 1) * size]
+
+    def mine(half):
+        return strips_ref.at[half * size : (half + 1) * size]
+
+    def send(source, spot, half, to):
         copy = pltpu.make_async_remote_copy(
             src_ref=source,
-            dst_ref=near_ref.at[spot, core],
+            dst_ref=part(spot, core, half),
             send_sem=send_sem.at[len(copies)],
-            recv_sem=recv_sem.at[spot, core],
+            recv_sem=recv_sem.at[spot, core, half],
             device_id={"tile": to},
             device_id_type=MESH,
         )
         copy.start()
         copies.append(copy)
 
-    def arrived(spot, side):
+    def arrived(spot, side, half):
         pltpu.make_async_remote_copy(
-            src_ref=strips_ref,
-            dst_ref=near_ref.at[spot, side],
+            src_ref=mine(half),
+            dst_ref=part(spot, side, half),
             send_sem=own_sem,
-            recv_sem=recv_sem.at[spot, side],
+            recv_sem=recv_sem.at[spot, side, half],
             device_id={"tile": partner},
             device_id_type=MESH,
         ).wait_recv()
 
-    def share(spot):
-        send(near_ref.at[spot, core], spot, partner)
-
-    send(strips_ref, 0, above)
-    send(strips_ref, 2 * PLANE, below)
-    for j in range(1, PLANE):
-        send(strips_ref, PLANE - j + PLANE * wraps[j], beside[j])
-    send(strips_ref, PLANE, partner)
-    arrived(0, core)
-    arrived(2 * PLANE, core)
-    for j in range(1, PLANE):
-        source = near_ref.at[2 * PLANE - 2 * PLANE * wraps[j], core]
-        send(source, 2 * PLANE - PLANE * wraps[j] - j, beside[j])
-    share(0)
-    share(2 * PLANE)
-    for j in range(1, PLANE):
-        spot = PLANE + j - PLANE * wraps[j]
-        arrived(spot, core)
-        share(spot)
-    for j in range(1, PLANE):
-        spot = j + PLANE * wraps[j]
-        arrived(spot, core)
-        share(spot)
-    for spot in range(2 * PLANE + 1):
-        arrived(spot, 1 - core)
+    def share(spot, half):
+        send(part(spot, core, half), spot, half, partner)
+
+    for half in range(HALVES):
+        send(mine(half), 0, half, above)
+        send(mine(half), 2 * PLANE, half, below)
+    for half in range(HALVES):
+        for j in range(1, PLANE):
+            send(mine(half), PLANE - j + PLANE * wraps[j], half, beside[j])
+        send(mine(half), PLANE, half, partner)
+    for half in range(HALVES):
+        arrived(0, core, half)
+        arrived(2 * PLANE, core, half)
+        for j in range(1, PLANE):
+            source = part(2 * PLANE - 2 * PLANE * wraps[j], core, half)
+            send(source, 2 * PLANE - PLANE * wraps[j] - j, half, beside[j])
+        share(0, half)
+        share(2 * PLANE, half)
+    for half in range(HALVES):
+        for j in range(1, PLANE):
+            spot = PLANE + j - PLANE * wraps[j]
+            arrived(spot, core, half)
+            share(spot, half)
+    for half in range(HALVES):
+        for j in range(1, PLANE):
+            spot = j + PLANE * wraps[j]
+            arrived(spot, core, half)
+            share(spot, half)
+    for half in range(HALVES):
+        for spot in range(2 * PLANE + 1):
+            arrived(spot, 1 - core, half)
     own.wait()
     for copy in copies:
         copy.wait_send()
@@ -525,8 +539,8 @@
         out_specs=hbm,
         scratch_shapes=[
             pltpu.SemaphoreType.DMA,
-            pltpu.SemaphoreType.DMA((4 * PLANE + 1,)),
-            pltpu.SemaphoreType.DMA((2 * PLANE + 1, 2)),
+            pltpu.SemaphoreType.DMA((HALVES * (4 * PLANE + 1),)),
+            pltpu.SemaphoreType.DMA((2 * PLANE + 1, 2, HALVES)),
         ],
         compiler_params=pltpu.CompilerParams(collective_id=0, has_side_effects=True),
     )(strips)

time: 27.5 us -> 27.7 us (level)
  no operation moved by 1% of the time
where the time goes in v3:
time: 27.7 us; the launch traced here: 27.5 us
  Pallas kernels  25.9 us (94%)
  local copies, waits for them, and re-layouts  1.5 us (5%)
    pallas_call x1, Pallas kernels, shards_fast(): pl.pallas_call(functools.partial(send_kernel, count), name='send', out_sh...  18.1 us
    pallas_call x1, Pallas kernels, shards_fast(): pl.pallas_call(solve_kernel, name='solve', out_shape=(jax.ShapeDtypeStruc...  5.37 us
    pallas_call x1, Pallas kernels, shards_fast(): pl.pallas_call(functools.partial(place_kernel, count), name='place', out_...  2.47 us
    unnamed x16, local copies, waits for them, and re-layouts  1.5 us

profile of v3, /device:TPU:0, one launch (start us, length us, event | category | flops | bytes accessed | tf_op | source)
XLA Modules:
  0.0 27.5 jit_solution(16994780496589865600)
XLA Ops:
  0.0 0.0 copy-start.2
  0.0 0.0 copy-start.4
  0.0 0.0 copy-start.3
  0.0 0.0 copy-start.7
  0.0 0.0 copy-start.6
  0.0 0.0 copy-start.5
  0.0 5.4 %solve.1 = (f32[24,8,1024]{2,1,0:T(8,128)}, f32[24,8,128]{2,1,0:T(8,128)}) custom-call(s32[2,4]{1,0:T(2,128)} %ec_ref.1, f32[24,4,2,900]{3,2,1,0:T(2,128)} %cot_hbm.1, f32[24,2,900]{2,1,0:T(2,128)} %cx_hbm.1, f32[24,2,900]{2,1,0:T(2,128)} %cy_hbm.1, f32[2,900]{1,0:T(2,128)} %dif_hbm.1, f32[24,2,900]{2,1,0:T(2,128)} %vd_hbm.1, s32[2,900]{1,0:T(2,128)} %lc_ref.1, ...), custom_call_target="tpu_custom_call" | custom-call | tf_op jit(solution)/shard_map/solve/pallas_call | solution.py:509
  5.4 0.0 copy-start.1
  5.4 18.1 %send.1.near_ref = f32[9,2,24,8,128]{4,3,2,1,0:T(8,128)} custom-call(f32[24,8,128]{2,1,0:T(8,128)} %get-tuple-element.7.strips_ref), custom_call_target="tpu_custom_call" | custom-call | tf_op jit(solution)/shard_map/send/pallas_call | solution.py:534
  23.5 0.0 copy-done.2
  23.5 0.0 copy-done.4
  23.5 0.0 copy-done.3
  23.6 0.0 copy-done.7
  23.6 0.0 copy-done.6
  23.6 0.0 copy-done.5
  23.6 0.0 copy-done.1
  23.6 0.0 copy-start
  23.6 1.5 %copy-done = f32[9,2,24,8,128]{4,3,2,1,0:T(8,128)S(1)} copy-done((f32[9,2,24,8,128]{4,3,2,1,0:T(8,128)S(1)}, f32[9,2,24,8,128]{4,3,2,1,0:T(8,128)}, u32[]{:S(2)}) %copy-start) | copy-done | bytes 1769496
  25.1 2.5 %place.1 = f32[24,4,2,900]{3,2,1,0:T(2,128)} custom-call(s32[2,4]{1,0:T(2,128)S(1)} %copy-done.5, s32[2,4]{1,0:T(2,128)S(1)} %copy-done.4, s32[2,4]{1,0:T(2,128)S(1)} %copy-done.6, s32[2,4]{1,0:T(2,128)S(1)} %copy-done.7, f32[9,2,24,8,128]{4,3,2,1,0:T(8,128)S(1)} %copy-done, f32[24,8,1024]{2,1,0:T(8,128)S(1)} %copy-done.1, s32[2,900]{1,0:T(2,128)S(1)} %copy-done.3, ...), custom_call_target="tpu_custom_call" | custom-call | tf_op jit(solution)/shard_map/place/pallas_call | solution.py:547
Async XLA Ops:
  0.0 23.5 %copy-start.2 = (bf16[128,1024]{1,0:T(8,128)(2,1)S(1)}, bf16[128,1024]{1,0:T(8,128)(2,1)}, u32[]{:S(2)}) copy-start(bf16[128,1024]{1,0:T(8,128)(2,1)} %constant.5.clone.place_ref) | copy-start | bytes 786436
  0.0 23.5 %copy-start.4 = (s32[2,4]{1,0:T(2,128)S(1)}, s32[2,4]{1,0:T(2,128)}, u32[]{:S(2)}) copy-start(s32[2,4]{1,0:T(2,128)} %ec_ref.1) | copy-start | bytes 100
  0.0 23.5 %copy-start.3 = (s32[2,900]{1,0:T(2,128)S(1)}, s32[2,900]{1,0:T(2,128)}, u32[]{:S(2)}) copy-start(s32[2,900]{1,0:T(2,128)} %lc_ref.1) | copy-start | bytes 21604
  0.0 23.6 %copy-start.7 = (s32[2,4]{1,0:T(2,128)S(1)}, s32[2,4]{1,0:T(2,128)}, u32[]{:S(2)}) copy-start(s32[2,4]{1,0:T(2,128)} %cc_ref.1) | copy-start | bytes 100
  0.0 23.6 %copy-start.6 = (s32[2,4]{1,0:T(2,128)S(1)}, s32[2,4]{1,0:T(2,128)}, u32[]{:S(2)}) copy-start(s32[2,4]{1,0:T(2,128)} %ct_ref.1) | copy-start | bytes 100
  0.0 23.6 %copy-start.5 = (s32[2,4]{1,0:T(2,128)S(1)}, s32[2,4]{1,0:T(2,128)}, u32[]{:S(2)}) copy-start(s32[2,4]{1,0:T(2,128)} %et_ref.1) | copy-start | bytes 100
  5.4 18.2 %copy-start.1 = (f32[24,8,1024]{2,1,0:T(8,128)S(1)}, f32[24,8,1024]{2,1,0:T(8,128)}, u32[]{:S(2)}) copy-start(f32[24,8,1024]{2,1,0:T(8,128)} %get-tuple-element.8.base_ref) | copy-start | bytes 2359300
  23.6 1.5 %copy-start = (f32[9,2,24,8,128]{4,3,2,1,0:T(8,128)S(1)}, f32[9,2,24,8,128]{4,3,2,1,0:T(8,128)}, u32[]{:S(2)}) copy-start(f32[9,2,24,8,128]{4,3,2,1,0:T(8,128)} %send.1.near_ref) | copy-start | bytes 5308420

commit v4 on v1

--- a/solution.py
+++ b/solution.py
@@ -369,11 +369,12 @@
         return 2 * lax.rem(chip + steps + chips, chips) + core
 
     partner = me + 1 - 2 * core
-    wraps = [(place + j) // PLANE for j in range(PLANE)]
-    beside = [at(j - PLANE * wraps[j]) for j in range(PLANE)]
+    dx = 1 - 2 * lax.rem(place, 2)
+    dy = 2 - 4 * (place // 2)
+    along_x, along_y = at(dx), at(dy)
     above, below = at(PLANE), at(-PLANE)
     barrier = pltpu.get_barrier_semaphore()
-    peers = [partner, above, below] + beside[1:]
+    peers = [partner, above, below, along_x, along_y]
     for peer in peers:
         pl.semaphore_signal(barrier, inc=1, device_id={"tile": peer}, device_id_type=MESH)
     own = pltpu.make_async_copy(strips_ref, near_ref.at[PLANE, core], own_sem)
@@ -406,24 +407,27 @@
     def share(spot):
         send(near_ref.at[spot, core], spot, partner)
 
+    def relay(spot, there, to):
+        send(near_ref.at[spot, core], there, to)
+
     send(strips_ref, 0, above)
     send(strips_ref, 2 * PLANE, below)
-    for j in range(1, PLANE):
-        send(strips_ref, PLANE - j + PLANE * wraps[j], beside[j])
+    send(strips_ref, PLANE - dx, along_x)
+    send(strips_ref, PLANE - dy, along_y)
     send(strips_ref, PLANE, partner)
+    arrived(PLANE + dx, core)
+    relay(PLANE + dx, PLANE + dx - dy, along_y)
+    share(PLANE + dx)
     arrived(0, core)
     arrived(2 * PLANE, core)
-    for j in range(1, PLANE):
-        source = near_ref.at[2 * PLANE - 2 * PLANE * wraps[j], core]
-        send(source, 2 * PLANE - PLANE * wraps[j] - j, beside[j])
+    relay(PLANE + 2 * dy, PLANE + dy, along_y)
+    relay(PLANE + 4 * dx, PLANE + 3 * dx, along_x)
     share(0)
     share(2 * PLANE)
-    for j in range(1, PLANE):
-        spot = PLANE + j - PLANE * wraps[j]
-        arrived(spot, core)
-        share(spot)
-    for j in range(1, PLANE):
-        spot = j + PLANE * wraps[j]
+    arrived(PLANE - dy, core)
+    relay(PLANE - dy, PLANE - dy - dx, along_x)
+    share(PLANE - dy)
+    for spot in (PLANE + dy, PLANE + dx + dy, PLANE - 3 * dx, PLANE - dy + dx):
         arrived(spot, core)
         share(spot)
     for spot in range(2 * PLANE + 1):

time: 27.5 us -> 30.1 us (1.095)
  Pallas kernels: 25.7 us -> 28.3 us
    pallas_call x1, Pallas kernels: 17.9 us -> 20.5 us  [shards_fast(): pl.pallas_call(functools.partial(send_kernel, count), name='send', out_sh...]
where the time goes in v4:
time: 30.1 us; the launch traced here: 29.9 us
  Pallas kernels  28.3 us (94%)
  local copies, waits for them, and re-layouts  1.5 us (5%)
    pallas_call x1, Pallas kernels, shards_fast(): pl.pallas_call(functools.partial(send_kernel, count), name='send', out_sh...  20.5 us
    pallas_call x1, Pallas kernels, shards_fast(): pl.pallas_call(solve_kernel, name='solve', out_shape=(jax.ShapeDtypeStruc...  5.37 us
    pallas_call x1, Pallas kernels, shards_fast(): pl.pallas_call(functools.partial(place_kernel, count), name='place', out_...  2.46 us
    unnamed x16, local copies, waits for them, and re-layouts  1.5 us

profile of v4, /device:TPU:0, one launch (start us, length us, event | category | flops | bytes accessed | tf_op | source)
XLA Modules:
  0.0 29.9 jit_solution(3001130533803590301)
XLA Ops:
  0.0 0.0 copy-start.2
  0.0 0.0 copy-start.4
  0.0 0.0 copy-start.3
  0.0 0.0 copy-start.7
  0.0 0.0 copy-start.6
  0.0 0.0 copy-start.5
  0.0 5.4 %solve.1 = (f32[24,8,1024]{2,1,0:T(8,128)}, f32[24,8,128]{2,1,0:T(8,128)}) custom-call(s32[2,4]{1,0:T(2,128)} %ec_ref.1, f32[24,4,2,900]{3,2,1,0:T(2,128)} %cot_hbm.1, f32[24,2,900]{2,1,0:T(2,128)} %cx_hbm.1, f32[24,2,900]{2,1,0:T(2,128)} %cy_hbm.1, f32[2,900]{1,0:T(2,128)} %dif_hbm.1, f32[24,2,900]{2,1,0:T(2,128)} %vd_hbm.1, s32[2,900]{1,0:T(2,128)} %lc_ref.1, ...), custom_call_target="tpu_custom_call" | custom-call | tf_op jit(solution)/shard_map/solve/pallas_call | solution.py:499
  5.4 0.0 copy-start.1
  5.4 20.5 %send.1.near_ref = f32[9,2,24,8,128]{4,3,2,1,0:T(8,128)} custom-call(f32[24,8,128]{2,1,0:T(8,128)} %get-tuple-element.7.strips_ref), custom_call_target="tpu_custom_call" | custom-call | tf_op jit(solution)/shard_map/send/pallas_call | solution.py:524
  25.9 0.0 copy-done.2
  25.9 0.0 copy-done.4
  25.9 0.0 copy-done.3
  25.9 0.0 copy-done.7
  26.0 0.0 copy-done.6
  26.0 0.0 copy-done.5
  26.0 0.0 copy-done.1
  26.0 0.0 copy-start
  26.0 1.5 %copy-done = f32[9,2,24,8,128]{4,3,2,1,0:T(8,128)S(1)} copy-done((f32[9,2,24,8,128]{4,3,2,1,0:T(8,128)S(1)}, f32[9,2,24,8,128]{4,3,2,1,0:T(8,128)}, u32[]{:S(2)}) %copy-start) | copy-done | bytes 1769496
  27.5 2.5 %place.1 = f32[24,4,2,900]{3,2,1,0:T(2,128)} custom-call(s32[2,4]{1,0:T(2,128)S(1)} %copy-done.5, s32[2,4]{1,0:T(2,128)S(1)} %copy-done.4, s32[2,4]{1,0:T(2,128)S(1)} %copy-done.6, s32[2,4]{1,0:T(2,128)S(1)} %copy-done.7, f32[9,2,24,8,128]{4,3,2,1,0:T(8,128)S(1)} %copy-done, f32[24,8,1024]{2,1,0:T(8,128)S(1)} %copy-done.1, s32[2,900]{1,0:T(2,128)S(1)} %copy-done.3, ...), custom_call_target="tpu_custom_call" | custom-call | tf_op jit(solution)/shard_map/place/pallas_call | solution.py:537
Async XLA Ops:
  0.0 25.9 %copy-start.2 = (bf16[128,1024]{1,0:T(8,128)(2,1)S(1)}, bf16[128,1024]{1,0:T(8,128)(2,1)}, u32[]{:S(2)}) copy-start(bf16[128,1024]{1,0:T(8,128)(2,1)} %constant.5.clone.place_ref) | copy-start | bytes 786436
  0.0 25.9 %copy-start.4 = (s32[2,4]{1,0:T(2,128)S(1)}, s32[2,4]{1,0:T(2,128)}, u32[]{:S(2)}) copy-start(s32[2,4]{1,0:T(2,128)} %ec_ref.1) | copy-start | bytes 100
  0.0 25.9 %copy-start.3 = (s32[2,900]{1,0:T(2,128)S(1)}, s32[2,900]{1,0:T(2,128)}, u32[]{:S(2)}) copy-start(s32[2,900]{1,0:T(2,128)} %lc_ref.1) | copy-start | bytes 21604
  0.0 25.9 %copy-start.7 = (s32[2,4]{1,0:T(2,128)S(1)}, s32[2,4]{1,0:T(2,128)}, u32[]{:S(2)}) copy-start(s32[2,4]{1,0:T(2,128)} %cc_ref.1) | copy-start | bytes 100
  0.0 25.9 %copy-start.6 = (s32[2,4]{1,0:T(2,128)S(1)}, s32[2,4]{1,0:T(2,128)}, u32[]{:S(2)}) copy-start(s32[2,4]{1,0:T(2,128)} %ct_ref.1) | copy-start | bytes 100
  0.0 26.0 %copy-start.5 = (s32[2,4]{1,0:T(2,128)S(1)}, s32[2,4]{1,0:T(2,128)}, u32[]{:S(2)}) copy-start(s32[2,4]{1,0:T(2,128)} %et_ref.1) | copy-start | bytes 100
  5.4 20.6 %copy-start.1 = (f32[24,8,1024]{2,1,0:T(8,128)S(1)}, f32[24,8,1024]{2,1,0:T(8,128)}, u32[]{:S(2)}) copy-start(f32[24,8,1024]{2,1,0:T(8,128)} %get-tuple-element.8.base_ref) | copy-start | bytes 2359300
  26.0 1.5 %copy-start = (f32[9,2,24,8,128]{4,3,2,1,0:T(8,128)S(1)}, f32[9,2,24,8,128]{4,3,2,1,0:T(8,128)}, u32[]{:S(2)}) copy-start(f32[9,2,24,8,128]{4,3,2,1,0:T(8,128)} %send.1.near_ref) | copy-start | bytes 5308420

commit v5 on v1

--- a/solution.py
+++ b/solution.py
@@ -411,6 +411,10 @@
     for j in range(1, PLANE):
         send(strips_ref, PLANE - j + PLANE * wraps[j], beside[j])
     send(strips_ref, PLANE, partner)
+    for j in range(1, PLANE):
+        spot = PLANE + j - PLANE * wraps[j]
+        arrived(spot, core)
+        share(spot)
     arrived(0, core)
     arrived(2 * PLANE, core)
     for j in range(1, PLANE):
@@ -418,10 +422,6 @@
         send(source, 2 * PLANE - PLANE * wraps[j] - j, beside[j])
     share(0)
     share(2 * PLANE)
-    for j in range(1, PLANE):
-        spot = PLANE + j - PLANE * wraps[j]
-        arrived(spot, core)
-        share(spot)
     for j in range(1, PLANE):
         spot = j + PLANE * wraps[j]
         arrived(spot, core)

time: 27.5 us -> 29 us (1.055)
  Pallas kernels: 25.7 us -> 27.2 us
    pallas_call x1, Pallas kernels: 17.9 us -> 19.4 us  [shards_fast(): pl.pallas_call(functools.partial(send_kernel, count), name='send', out_sh...]
where the time goes in v5:
time: 29 us; the launch traced here: 28.8 us
  Pallas kernels  27.2 us (94%)
  local copies, waits for them, and re-layouts  1.5 us (5%)
    pallas_call x1, Pallas kernels, shards_fast(): pl.pallas_call(functools.partial(send_kernel, count), name='send', out_sh...  19.4 us
    pallas_call x1, Pallas kernels, shards_fast(): pl.pallas_call(solve_kernel, name='solve', out_shape=(jax.ShapeDtypeStruc...  5.37 us
    pallas_call x1, Pallas kernels, shards_fast(): pl.pallas_call(functools.partial(place_kernel, count), name='place', out_...  2.46 us
    unnamed x16, local copies, waits for them, and re-layouts  1.5 us

profile of v5, /device:TPU:0, one launch (start us, length us, event | category | flops | bytes accessed | tf_op | source)
XLA Modules:
  0.0 28.8 jit_solution(17018898059306265033)
XLA Ops:
  0.0 0.0 copy-start.2
  0.0 0.0 copy-start.4
  0.0 0.0 copy-start.3
  0.0 0.0 copy-start.7
  0.0 0.0 copy-start.6
  0.0 0.0 copy-start.5
  0.0 5.4 %solve.1 = (f32[24,8,1024]{2,1,0:T(8,128)}, f32[24,8,128]{2,1,0:T(8,128)}) custom-call(s32[2,4]{1,0:T(2,128)} %ec_ref.1, f32[24,4,2,900]{3,2,1,0:T(2,128)} %cot_hbm.1, f32[24,2,900]{2,1,0:T(2,128)} %cx_hbm.1, f32[24,2,900]{2,1,0:T(2,128)} %cy_hbm.1, f32[2,900]{1,0:T(2,128)} %dif_hbm.1, f32[24,2,900]{2,1,0:T(2,128)} %vd_hbm.1, s32[2,900]{1,0:T(2,128)} %lc_ref.1, ...), custom_call_target="tpu_custom_call" | custom-call | tf_op jit(solution)/shard_map/solve/pallas_call | solution.py:495
  5.4 0.0 copy-start.1
  5.4 19.4 %send.1.near_ref = f32[9,2,24,8,128]{4,3,2,1,0:T(8,128)} custom-call(f32[24,8,128]{2,1,0:T(8,128)} %get-tuple-element.7.strips_ref), custom_call_target="tpu_custom_call" | custom-call | tf_op jit(solution)/shard_map/send/pallas_call | solution.py:520
  24.8 0.0 copy-done.2
  24.8 0.0 copy-done.4
  24.8 0.0 copy-done.3
  24.8 0.0 copy-done.7
  24.8 0.0 copy-done.6
  24.8 0.0 copy-done.5
  24.8 0.0 copy-done.1
  24.9 0.0 copy-start
  24.9 1.5 %copy-done = f32[9,2,24,8,128]{4,3,2,1,0:T(8,128)S(1)} copy-done((f32[9,2,24,8,128]{4,3,2,1,0:T(8,128)S(1)}, f32[9,2,24,8,128]{4,3,2,1,0:T(8,128)}, u32[]{:S(2)}) %copy-start) | copy-done | bytes 1769496
  26.3 2.5 %place.1 = f32[24,4,2,900]{3,2,1,0:T(2,128)} custom-call(s32[2,4]{1,0:T(2,128)S(1)} %copy-done.5, s32[2,4]{1,0:T(2,128)S(1)} %copy-done.4, s32[2,4]{1,0:T(2,128)S(1)} %copy-done.6, s32[2,4]{1,0:T(2,128)S(1)} %copy-done.7, f32[9,2,24,8,128]{4,3,2,1,0:T(8,128)S(1)} %copy-done, f32[24,8,1024]{2,1,0:T(8,128)S(1)} %copy-done.1, s32[2,900]{1,0:T(2,128)S(1)} %copy-done.3, ...), custom_call_target="tpu_custom_call" | custom-call | tf_op jit(solution)/shard_map/place/pallas_call | solution.py:533
Async XLA Ops:
  0.0 24.8 %copy-start.2 = (bf16[128,1024]{1,0:T(8,128)(2,1)S(1)}, bf16[128,1024]{1,0:T(8,128)(2,1)}, u32[]{:S(2)}) copy-start(bf16[128,1024]{1,0:T(8,128)(2,1)} %constant.5.clone.place_ref) | copy-start | bytes 786436
  0.0 24.8 %copy-start.4 = (s32[2,4]{1,0:T(2,128)S(1)}, s32[2,4]{1,0:T(2,128)}, u32[]{:S(2)}) copy-start(s32[2,4]{1,0:T(2,128)} %ec_ref.1) | copy-start | bytes 100
  0.0 24.8 %copy-start.3 = (s32[2,900]{1,0:T(2,128)S(1)}, s32[2,900]{1,0:T(2,128)}, u32[]{:S(2)}) copy-start(s32[2,900]{1,0:T(2,128)} %lc_ref.1) | copy-start | bytes 21604
  0.0 24.8 %copy-start.7 = (s32[2,4]{1,0:T(2,128)S(1)}, s32[2,4]{1,0:T(2,128)}, u32[]{:S(2)}) copy-start(s32[2,4]{1,0:T(2,128)} %cc_ref.1) | copy-start | bytes 100
  0.0 24.8 %copy-start.6 = (s32[2,4]{1,0:T(2,128)S(1)}, s32[2,4]{1,0:T(2,128)}, u32[]{:S(2)}) copy-start(s32[2,4]{1,0:T(2,128)} %ct_ref.1) | copy-start | bytes 100
  0.0 24.8 %copy-start.5 = (s32[2,4]{1,0:T(2,128)S(1)}, s32[2,4]{1,0:T(2,128)}, u32[]{:S(2)}) copy-start(s32[2,4]{1,0:T(2,128)} %et_ref.1) | copy-start | bytes 100
  5.4 19.4 %copy-start.1 = (f32[24,8,1024]{2,1,0:T(8,128)S(1)}, f32[24,8,1024]{2,1,0:T(8,128)}, u32[]{:S(2)}) copy-start(f32[24,8,1024]{2,1,0:T(8,128)} %get-tuple-element.8.base_ref) | copy-start | bytes 2359300
  24.9 1.5 %copy-start = (f32[9,2,24,8,128]{4,3,2,1,0:T(8,128)S(1)}, f32[9,2,24,8,128]{4,3,2,1,0:T(8,128)}, u32[]{:S(2)}) copy-start(f32[9,2,24,8,128]{4,3,2,1,0:T(8,128)} %send.1.near_ref) | copy-start | bytes 5308420
